TPU v7x, 128 devices: a whole 4x4x4 slice. The times are simulated.
128 devices in a mesh: req: 32 (over z, x, core), tp: 4 (over y).
Axes of the slice: x: 4, y: 4, z: 4, core: 2. Of those that a mesh axis runs over, the one named last changes fastest.
Arguments:
- tokens: bfloat16 [12288, 5120], P('req'), may hold values from -40 to 40
- w_query: bfloat16 [5120, 2560], P(None, 'tp'), may hold values from -0.125 to 0.125
- query_bias: float32 [2560], P('tp'), may hold values from -24 to 24
- w_keyval: bfloat16 [5120, 1024], P(None, 'tp'), may hold values from -0.21875 to 0.21875
- keyval_bias: float32 [1024], P('tp'), may hold values from -2.5 to 2.5
- w_out: bfloat16 [2560, 5120], P('tp'), may hold values from -0.25 to 0.25
- attn_gain: float32 [5120], replicated, may hold values from 0.25 to 1.75
- final_norm_gain: float32 [5120], replicated, may hold values from 0.25 to 1.75
- head_weight: bfloat16 [5120, 76032], P(None, ('req', 'tp')), may hold values from -0.25 to 0.25
- kv_pool: bfloat16 [851968, 4, 256], P('req', 'tp'), may hold values from -17 to 17
- cache_len: int32 [512], replicated, may hold values from 256 to 3072, as said below
Outputs:
- states: bfloat16 [12288, 5120], P('req', 'tp')
- new_kv: bfloat16 [12288, 4, 256], P('req', 'tp')
- row_norms: float32 [512], P('req')
- logit_max: float32 [512], replicated
- logits: float32 [512, 76032], P(None, ('req', 'tp'))
Inputs may be any that keep to these rules, and one draw needn't show every extreme that they name: `cache_len`: every cache holds 256 or 3072 rows. Exactly 64 requests hold 3072; requests i * 16 to i * 16 + 15 hold at most 8 of them for every i, and exactly 8 for some i, so their caches fill at most 26624 rows, and exactly 26624 for some i.
All inputs are finite; a program needn't handle non-finite values.
Results may differ from a plain program's by a relative error of at most 0.014.
Values may be sent and summed in bfloat16 or wider, within the bound.
A program may use at most 192 MiB of HBM per device.

v0:
```python
import math
import jax
import jax.numpy as jnp
from jax import lax
from jax.sharding import PartitionSpec as P

HD = 128
GROUP = 5
NEW = 24
LONG = 3072
THETA = 1000000.0
EPS = 1e-06
NEG = -1e30


def rope_rotate(vectors, positions):
    head_width = vectors.shape[-1]
    halfway = head_width // 2
    frequency = THETA ** (-(jnp.arange(halfway, dtype=jnp.float32) * (2.0 / head_width)))
    angles = positions[..., None] * frequency
    cosine = jnp.cos(angles)
    sine_part = jnp.sin(angles)
    front_part = vectors[..., :halfway]
    back_part = vectors[..., halfway:]
    return jnp.concatenate(
        [front_part * cosine - back_part * sine_part, back_part * cosine + front_part * sine_part],
        axis=-1,
    )


def online_update(state_in, scores, value_matrix):
    running_max, totals, weighted = state_in
    new_max = jnp.maximum(running_max, jnp.max(scores, axis=-1))
    rescale = jnp.exp(running_max - new_max)
    weight_matrix = jnp.exp(scores - new_max[..., None])
    totals = totals * rescale + jnp.sum(weight_matrix, axis=-1)
    weighted = weighted * rescale[..., None] + jnp.einsum(
        "amz,zav->amv",
        weight_matrix.astype(jnp.bfloat16),
        value_matrix,
        preferred_element_type=jnp.float32,
    )
    return (new_max, totals, weighted)


def attend_windows(query_rows, pool_part, leading_row, req_starts, req_lens, start_state):
    head_width = query_rows.shape[-1]
    kv_local = query_rows.shape[0]
    query_count = query_rows.shape[1]
    req_count = req_starts.shape[0]
    row_span = query_count // req_count
    part_rows = pool_part.shape[0]
    window_rows = min(LONG, part_rows)
    batch_size = math.gcd(req_count, 4)
    batch_count = req_count // batch_size

    def per_request(query_block, begin, length, state_max, state_totals, state_weighted):
        first = jnp.clip(begin - leading_row, 0, part_rows - window_rows)
        window = lax.dynamic_slice_in_dim(pool_part, first, window_rows, 0)
        row_index = leading_row + first + jnp.arange(window_rows, dtype=jnp.int32)
        inside = (row_index >= begin) & (row_index < begin + length)
        scores = jnp.einsum(
            "mjl,wml->mjw",
            query_block,
            window[..., :head_width],
            preferred_element_type=jnp.float32,
        )
        scores = jnp.where(inside[None, None, :], scores, -jnp.inf)
        return online_update(
            (state_max, state_totals, state_weighted), scores, window[..., head_width:]
        )

    def split_requests(array_in):
        moved = jnp.moveaxis(
            array_in.reshape((kv_local, req_count, row_span) + array_in.shape[2:]), 1, 0
        )
        return moved.reshape((batch_count, batch_size) + moved.shape[1:])

    def join_requests(array_in):
        merged = array_in.reshape((req_count,) + array_in.shape[2:])
        return jnp.moveaxis(merged, 0, 1).reshape((kv_local, query_count) + merged.shape[3:])

    def one_batch(inputs):
        return jax.vmap(per_request)(*inputs)

    batched = (
        split_requests(query_rows),
        req_starts.reshape(batch_count, batch_size),
        req_lens.reshape(batch_count, batch_size),
        split_requests(start_state[0]),
        split_requests(start_state[1]),
        split_requests(start_state[2]),
    )
    result = lax.map(one_batch, batched)
    return tuple((join_requests(part_state) for part_state in result))


def local(
    tokens,
    w_query,
    query_bias,
    w_keyval,
    keyval_bias,
    w_out,
    attn_gain,
    final_norm_gain,
    head_weight,
    kv_pool,
    cache_len,
):
    groups = lax.axis_size("req")
    my_group = lax.axis_index("req")
    tp_count = lax.axis_size("tp")
    tp_index = lax.axis_index("tp")
    tok_rows = tokens.shape[0]
    model_width = tokens.shape[1]
    per_group = tok_rows // NEW
    kv_local = kv_pool.shape[1]
    lens_grid = cache_len.reshape(groups, per_group)
    my_lens = lax.dynamic_slice_in_dim(lens_grid, my_group, 1, 0)[0]
    my_starts = jnp.cumsum(my_lens) - my_lens
    source = tokens.astype(jnp.float32)
    mean_square = jnp.mean(source * source, axis=1, keepdims=True)
    normed = (source / jnp.sqrt(mean_square + EPS) * attn_gain[None, :]).astype(jnp.bfloat16)
    query_raw = jnp.dot(normed, w_query, preferred_element_type=jnp.float32) + query_bias[None, :]
    keyval_raw = (
        jnp.dot(normed, w_keyval, preferred_element_type=jnp.float32) + keyval_bias[None, :]
    )
    positions = (my_lens[:, None] + jnp.arange(NEW, dtype=jnp.int32)[None, :]).astype(jnp.float32)
    query_heads = query_raw.reshape(per_group, NEW, kv_local, GROUP, HD)
    queries = (
        rope_rotate(query_heads, positions[:, :, None, None]) * (1.0 / math.sqrt(HD))
    ).astype(jnp.bfloat16)
    keyval_heads = keyval_raw.reshape(per_group, NEW, kv_local, 2, HD)
    key_new = rope_rotate(keyval_heads[:, :, :, 0, :], positions[:, :, None]).astype(jnp.bfloat16)
    value_new = keyval_heads[:, :, :, 1, :].astype(jnp.bfloat16)
    new_kv = jnp.concatenate([key_new, value_new], axis=-1).reshape(tok_rows, kv_local, 2 * HD)
    row_span = NEW * GROUP
    query_count = per_group * row_span
    query_rows = jnp.transpose(queries, (2, 0, 1, 3, 4)).reshape(kv_local, query_count, HD)
    start_state = (
        jnp.full((kv_local, query_count), NEG, jnp.float32),
        jnp.zeros((kv_local, query_count), jnp.float32),
        jnp.zeros((kv_local, query_count, HD), jnp.float32),
    )
    carry_state = attend_windows(query_rows, kv_pool, 0, my_starts, my_lens, start_state)
    key_rows = key_new.reshape(tok_rows, kv_local, HD)
    value_rows = value_new.reshape(tok_rows, kv_local, HD)
    new_scores = jnp.einsum(
        "kqd,mkd->kqm", query_rows, key_rows, preferred_element_type=jnp.float32
    )
    query_token = jnp.arange(query_count, dtype=jnp.int32) // GROUP
    key_token = jnp.arange(tok_rows, dtype=jnp.int32)
    allowed = (query_token[:, None] // NEW == key_token[None, :] // NEW) & (
        key_token[None, :] <= query_token[:, None]
    )
    new_scores = jnp.where(allowed[None], new_scores, -jnp.inf)
    carry_state = online_update(carry_state, new_scores, value_rows)
    attention = (carry_state[2] / carry_state[1][..., None]).astype(jnp.bfloat16)
    attention = jnp.transpose(
        attention.reshape(kv_local, per_group, NEW, GROUP, HD), (1, 2, 0, 3, 4)
    ).reshape(tok_rows, kv_local * GROUP * HD)
    partial_value = jnp.dot(attention, w_out, preferred_element_type=jnp.float32)
    width_local = model_width // tp_count
    summed = lax.psum(partial_value.astype(jnp.bfloat16), "tp").astype(jnp.float32)
    states_full = (source + summed).astype(jnp.bfloat16)
    states = lax.dynamic_slice_in_dim(states_full, tp_index * width_local, width_local, 1)
    last_rows = states_full.reshape(per_group, NEW, model_width)[:, NEW - 1, :].astype(jnp.float32)
    row_norms = jnp.sqrt(jnp.mean(last_rows * last_rows, axis=1) + EPS)
    final_rows = (last_rows / row_norms[:, None] * final_norm_gain[None, :]).astype(jnp.bfloat16)
    logits = jnp.dot(
        lax.all_gather(final_rows, "req", axis=0, tiled=True),
        head_weight,
        preferred_element_type=jnp.float32,
    )
    logit_max = lax.pmax(jnp.max(logits, axis=1), ("req", "tp"))
    return (states, new_kv, row_norms, logit_max, logits)


def solution(mesh):
    return jax.shard_map(
        local,
        mesh=mesh,
        in_specs=(
            P("req", None),
            P(None, "tp"),
            P("tp"),
            P(None, "tp"),
            P("tp"),
            P("tp", None),
            P(),
            P(),
            P(None, ("req", "tp")),
            P("req", "tp", None),
            P(),
        ),
        out_specs=(P("req", "tp"), P("req", "tp", None), P("req"), P(), P(None, ("req", "tp"))),
        check_vma=False,
    )
```

profile of v0, /device:TPU:1, one launch (start us, length us, event | category | flops | bytes accessed | tf_op | source)
XLA Modules:
  0.0 365.2 jit_solution(11805179985593253152)
XLA Ops:
  7.3 3.1 fusion.27
  10.7 3.6 fusion.29
  16.1 4.2 %convolution_add_fusion.1 = f32[384,640]{1,0:T(8,128)} fusion(bf16[384,5120]{1,0:T(8,128)(2,1)S(1)} %fusion.29, bf16[5120,640]{1,0:T(8,128)(2,1)S(1)} %copy-done.12, f32[640]{0:T(1024)S(1)} %copy-done.13), kind=kOutput, calls=%fused_computation.58 | convolution fusion | flops 2516828160 | bytes 11471360 | tf_op jit(solution)/shard_map/dot_general | solution.py:125
  23.5 4.2 %multiply_subtract_fusion = (f32[16,24,1,5,64]{4,3,1,0,2:T(8,128)}, f32[16,24,1,5,64]{4,3,1,0,2:T(8,128)}) fusion(f32[16,24,1,5,128]{4,3,1,0,2:T(8,128)} %reshape.555, f32[16,24,64]{2,1,0:T(8,128)S(1)} %get-tuple-element.120, f32[16,24,64]{2,1,0:T(8,128)S(1)} %get-tuple-element.119), kind=kLoop, calls=%fused_computation.56 | loop fusion | flops 737280 | bytes 2162688 | tf_op jit(solution)/shard_map/sub | solution.py:26
  38.9 3.3 convolution_add_fusion.2
  45.7 81.0 %while.17 = (s32[]{:T(128)}, f32[4,4,1,120]{3,1,2,0:T(4,128)S(1)}, f32[4,4,1,120]{3,1,2,0:T(4,128)S(1)}, f32[4,4,1,120,128]{4,3,1,2,0:T(8,128)}, s32[4,4]{1,0:T(...) while((s32[]{:T(128)}, f32[4,4,1,120]{3,1,2,0:T(4,128)S(1)}, ...), condition=%wide.region_5.6_spmd, body=%wide.region_2.5_spmd.sunk | while | flops 766884224 | bytes 52985684 | solution.py:94
  46.1 12.2 %while.18 = (s32[]{:T(128)}, bf16[26624,1,256]{2,0,1:T(8,128)(2,1)}, s32[4,3]{1,0:T(4,128)S(1)}, bf16[4,3072,1,256]{3,1,2,0:T(8,128)(2,1)}, s32[]{:T(128)}) while((s32[]{:T(128)}, bf16[26624,1,256]{2,0,1:T(8,128)(2,1)}, s32[4,3]{1,0:T(4,128)S(1)}, bf16[4,3072,1,256]{3,1,2,0:T(8,128)(2,1)}, s32[]{:T(128)}) %tuple.62), condition=%wide.while_cond, body=%wide.while_body.sunk | while | flops 2 | bytes 3145833 | solution.py:59
  46.1 3.2 bitcast_dynamic-update-slice_fusion.3
  55.3 3.0 bitcast_dynamic-update-slice_fusion.3
  58.3 4.2 %select_reduce_fusion.2 = (f32[4,120]{1,0:T(4,128)S(1)}, f32[4,120,3072]{2,1,0:T(8,128)S(1)}) fusion(pred[4,3072]{1,0:T(4,128)(4,1)S(1)} %fusion.90, bf16[4,3072,1,256]{3,1,0,2:T(8,128)(2,1)} %bitcast.118, bf16[1,4,1,120,128]{4,1,0,3,2:T(4,128)(2,1)S(1)} %constant_dynamic-slice_fusion.8), kind=kOutput, calls=%fused_computation.3.clone.1 | convolution fusion | flops 380436000 | bytes 9181056 | tf_op jit(solution)/shard_map/while/body/eval_jaxpr/vmap(mjl,wml->mjw)/dot_general | solution.py:62
  66.4 12.1 %while.18 = (s32[]{:T(128)}, bf16[26624,1,256]{2,0,1:T(8,128)(2,1)}, s32[4,3]{1,0:T(4,128)S(1)}, bf16[4,3072,1,256]{3,1,2,0:T(8,128)(2,1)}, s32[]{:T(128)}) while((s32[]{:T(128)}, bf16[26624,1,256]{2,0,1:T(8,128)(2,1)}, s32[4,3]{1,0:T(4,128)S(1)}, bf16[4,3072,1,256]{3,1,2,0:T(8,128)(2,1)}, s32[]{:T(128)}) %tuple.62), condition=%wide.while_cond, body=%wide.while_body.sunk | while | flops 2 | bytes 3145833 | solution.py:59
  75.4 3.0 bitcast_dynamic-update-slice_fusion.3
  78.4 4.2 %select_reduce_fusion.2 = (f32[4,120]{1,0:T(4,128)S(1)}, f32[4,120,3072]{2,1,0:T(8,128)S(1)}) fusion(pred[4,3072]{1,0:T(4,128)(4,1)S(1)} %fusion.90, bf16[4,3072,1,256]{3,1,0,2:T(8,128)(2,1)} %bitcast.118, bf16[1,4,1,120,128]{4,1,0,3,2:T(4,128)(2,1)S(1)} %constant_dynamic-slice_fusion.8), kind=kOutput, calls=%fused_computation.3.clone.1 | convolution fusion | flops 380436000 | bytes 9181056 | tf_op jit(solution)/shard_map/while/body/eval_jaxpr/vmap(mjl,wml->mjw)/dot_general | solution.py:62
  86.5 12.1 %while.18 = (s32[]{:T(128)}, bf16[26624,1,256]{2,0,1:T(8,128)(2,1)}, s32[4,3]{1,0:T(4,128)S(1)}, bf16[4,3072,1,256]{3,1,2,0:T(8,128)(2,1)}, s32[]{:T(128)}) while((s32[]{:T(128)}, bf16[26624,1,256]{2,0,1:T(8,128)(2,1)}, s32[4,3]{1,0:T(4,128)S(1)}, bf16[4,3072,1,256]{3,1,2,0:T(8,128)(2,1)}, s32[]{:T(128)}) %tuple.62), condition=%wide.while_cond, body=%wide.while_body.sunk | while | flops 2 | bytes 3145833 | solution.py:59
  95.6 3.0 bitcast_dynamic-update-slice_fusion.3
  98.6 4.2 %select_reduce_fusion.2 = (f32[4,120]{1,0:T(4,128)S(1)}, f32[4,120,3072]{2,1,0:T(8,128)S(1)}) fusion(pred[4,3072]{1,0:T(4,128)(4,1)S(1)} %fusion.90, bf16[4,3072,1,256]{3,1,0,2:T(8,128)(2,1)} %bitcast.118, bf16[1,4,1,120,128]{4,1,0,3,2:T(4,128)(2,1)S(1)} %constant_dynamic-slice_fusion.8), kind=kOutput, calls=%fused_computation.3.clone.1 | convolution fusion | flops 380436000 | bytes 9181056 | tf_op jit(solution)/shard_map/while/body/eval_jaxpr/vmap(mjl,wml->mjw)/dot_general | solution.py:62
  106.7 12.1 %while.18 = (s32[]{:T(128)}, bf16[26624,1,256]{2,0,1:T(8,128)(2,1)}, s32[4,3]{1,0:T(4,128)S(1)}, bf16[4,3072,1,256]{3,1,2,0:T(8,128)(2,1)}, s32[]{:T(128)}) while((s32[]{:T(128)}, bf16[26624,1,256]{2,0,1:T(8,128)(2,1)}, s32[4,3]{1,0:T(4,128)S(1)}, bf16[4,3072,1,256]{3,1,2,0:T(8,128)(2,1)}, s32[]{:T(128)}) %tuple.62), condition=%wide.while_cond, body=%wide.while_body.sunk | while | flops 2 | bytes 3145833 | solution.py:59
  118.7 4.2 %select_reduce_fusion.2 = (f32[4,120]{1,0:T(4,128)S(1)}, f32[4,120,3072]{2,1,0:T(8,128)S(1)}) fusion(pred[4,3072]{1,0:T(4,128)(4,1)S(1)} %fusion.90, bf16[4,3072,1,256]{3,1,0,2:T(8,128)(2,1)} %bitcast.118, bf16[1,4,1,120,128]{4,1,0,3,2:T(4,128)(2,1)S(1)} %constant_dynamic-slice_fusion.8), kind=kOutput, calls=%fused_computation.3.clone.1 | convolution fusion | flops 380436000 | bytes 9181056 | tf_op jit(solution)/shard_map/while/body/eval_jaxpr/vmap(mjl,wml->mjw)/dot_general | solution.py:62
  129.9 7.6 %convolution_convert_fusion = bf16[384,5120]{1,0:T(8,128)(2,1)} fusion(bf16[384,640]{1,0:T(8,128)(2,1)S(1)} %reshape_transpose_reshape.16, bf16[640,5120]{1,0:T(8,128)(2,1)} %param.18), kind=kOutput, calls=%fused_computation.45 | convolution fusion | flops 2518548480 | bytes 10977280 | tf_op jit(solution)/shard_map/dot_general | solution.py:163
  137.5 91.8 %all-reduce.3.cloned.1.call-done = bf16[384,5120]{1,0:T(8,128)(2,1)} async-done(((bf16[384,5120]{1,0:T(8,128)(2,1)}), bf16[384,5120]{1,0:T(8,128)(2,1)}) %all-reduce.3.cloned.1.call-update) | async-done | bytes 3932176 | tf_op jit(solution)/shard_map/psum | solution.py:165
  229.4 4.8 %fusion.30 = bf16[384,5120]{1,0:T(8,128)(2,1)S(1)} fusion(bf16[384,5120]{1,0:T(8,128)(2,1)} %param.13, bf16[384,5120]{1,0:T(8,128)(2,1)} %all-reduce.3.cloned.1.call-done), kind=kLoop, calls=%fused_computation.44 | loop fusion | flops 7864320 | bytes 11796480 | tf_op jit(solution)/shard_map/convert_element_type | solution.py:166
  240.4 44.9 %all-gather.2.cloned.1.call-done = bf16[512,5120]{1,0:T(8,128)(2,1)} async-done(((bf16[16,5120]{1,0:T(8,128)(2,1)}), bf16[512,5120]{1,0:T(8,128)(2,1)}) %all-gather.2.cloned.1.call-update) | async-done | bytes 5242896 | tf_op jit(solution)/shard_map/all_gather | solution.py:172
  285.3 8.8 %fusion.72 = (f32[512]{0:T(512)S(1)}, f32[512,594]{0,1:T(8,128)}) fusion(bf16[512,5120]{1,0:T(8,128)(2,1)} %all-gather.2.cloned.1.call-done, bf16[5120,594]{0,1:T(8,128)(2,1)} %param.21), kind=kOutput, calls=%fused_computation.122 | convolution fusion | flops 3114574336 | bytes 12544000 | tf_op jit(solution)/shard_map/dot_general | solution.py:171
  294.2 64.1 %pmax.7 = f32[512]{0:T(512)} all-reduce(f32[512]{0:T(512)S(1)} %get-tuple-element.123), channel_id=1, replica_groups=mesh['req'=32,'tp'=4] {'req','tp'}, use_global_device_ids=true, to_apply=%region_11.12 | all-reduce | flops 512 | bytes 4096 | tf_op jit(solution)/shard_map/pmax | solution.py:176
  (158 shorter events, 80.7 us)
Async XLA Ops:
  7.2 31.7 %copy-start = (bf16[5120,256]{1,0:T(8,128)(2,1)S(1)}, bf16[5120,256]{1,0:T(8,128)(2,1)}, u32[]{:S(2)}) copy-start(bf16[5120,256]{1,0:T(8,128)(2,1)} %param.16) | copy-start | bytes 7864324
  7.2 3.3 copy-start.10
  7.2 3.5 copy-start.8
  7.2 222.2 %all-reduce.3.cloned.1.call-start = ((), (), s32[]{:S(2)}) async-start(), calls=%async_computation | async-start | bytes 7864320 | tf_op jit(solution)/shard_map/psum | solution.py:165
  10.6 5.5 %copy-start.12 = (bf16[5120,640]{1,0:T(8,128)(2,1)S(1)}, bf16[5120,640]{1,0:T(8,128)(2,1)}, u32[]{:S(2)}) copy-start(bf16[5120,640]{1,0:T(8,128)(2,1)} %param.14) | copy-start | bytes 19660804
  10.7 5.5 %copy-start.13 = (f32[640]{0:T(1024)S(1)}, f32[640]{0:T(1024)}, u32[]{:S(2)}) copy-start(f32[640]{0:T(1024)} %param.15) | copy-start | bytes 7684
  14.2 1.9 copy-start.4
  30.1 8.8 %copy-start.14 = (f32[256]{0:T(256)S(1)}, f32[256]{0:T(256)}, u32[]{:S(2)}) copy-start(f32[256]{0:T(256)} %param.17) | copy-start | bytes 3076
  45.7 81.2 %copy-start.5 = (f32[1920,64]{1,0:T(8,128)S(1)}, f32[1920,64]{1,0:T(8,128)}, u32[]{:S(2)}) copy-start(f32[1920,64]{1,0:T(8,128)} %concatenate.59) | copy-start | bytes 1474564
  45.7 81.2 %copy-start.6 = (f32[1920,64]{1,0:T(8,128)S(1)}, f32[1920,64]{1,0:T(8,128)}, u32[]{:S(2)}) copy-start(f32[1920,64]{1,0:T(8,128)} %concatenate.60) | copy-start | bytes 1474564
  58.3 4.3 %copy-start.2 = (bf16[4,3072,1,256]{3,1,2,0:T(8,128)(2,1)S(1)}, bf16[4,3072,1,256]{3,1,2,0:T(8,128)(2,1)}, u32[]{:S(2)}) copy-start(bf16[4,3072,1,256]{3,1,2,0:T(8,128)(2,1)} %get-tuple-element.216) | copy-start | bytes 18874372 | tf_op jit(solution)/shard_map/while
  78.4 4.2 %copy-start.2 = (bf16[4,3072,1,256]{3,1,2,0:T(8,128)(2,1)S(1)}, bf16[4,3072,1,256]{3,1,2,0:T(8,128)(2,1)}, u32[]{:S(2)}) copy-start(bf16[4,3072,1,256]{3,1,2,0:T(8,128)(2,1)} %get-tuple-element.216) | copy-start | bytes 18874372 | tf_op jit(solution)/shard_map/while
  98.6 4.2 %copy-start.2 = (bf16[4,3072,1,256]{3,1,2,0:T(8,128)(2,1)S(1)}, bf16[4,3072,1,256]{3,1,2,0:T(8,128)(2,1)}, u32[]{:S(2)}) copy-start(bf16[4,3072,1,256]{3,1,2,0:T(8,128)(2,1)} %get-tuple-element.216) | copy-start | bytes 18874372 | tf_op jit(solution)/shard_map/while
  118.7 4.2 %copy-start.2 = (bf16[4,3072,1,256]{3,1,2,0:T(8,128)(2,1)S(1)}, bf16[4,3072,1,256]{3,1,2,0:T(8,128)(2,1)}, u32[]{:S(2)}) copy-start(bf16[4,3072,1,256]{3,1,2,0:T(8,128)(2,1)} %get-tuple-element.216) | copy-start | bytes 18874372 | tf_op jit(solution)/shard_map/while
  126.9 1.5 copy-start.7
  137.5 99.1 %copy-start.9 = (f32[5120]{0:T(1024)S(1)}, f32[5120]{0:T(1024)}, u32[]{:S(2)}) copy-start(f32[5120]{0:T(1024)} %param.20) | copy-start | bytes 61444
  137.5 147.8 %all-gather.2.cloned.1.call-start = ((), (), s32[]{:S(2)}) async-start(), calls=%async_computation.1 | async-start | bytes 5406720 | tf_op jit(solution)/shard_map/all_gather | solution.py:172
  234.2 1.9 copy-start.3
  236.6 57.6 %copy-start.11 = (f32[16]{0:T(128)}, f32[16]{0:T(128)S(1)}, u32[]{:S(2)}) copy-start(f32[16]{0:T(128)S(1)} %add_sqrt_fusion.1) | copy-start | bytes 196
  285.3 73.0 %copy-start.1 = (bf16[5120,256]{1,0:T(8,128)(2,1)S(1)}, bf16[5120,256]{1,0:T(8,128)(2,1)}, u32[]{:S(2)}) copy-start(bf16[5120,256]{1,0:T(8,128)(2,1)} %param.16) | copy-start | bytes 7864324
Sparse Core Ops, SparseCore 0:
  137.6 91.7 all-reduce.2
  237.5 47.7 all-gather.1
where the time goes:
time: 366 us; the launch traced here: 365 us
  waiting for transfers between devices  137 us (37%)
  local copies, waits for them, and re-layouts  69.7 us (19%)
  blocking collectives  64.1 us (18%)
  matrix products  51.4 us (14%)
  other arithmetic  28.1 us (8%)
  between operations  14.4 us (4%)
    psum x1, waiting for transfers between devices, local(): lax.psum(partial_value.astype(jnp.bfloat16), 'tp').astype(jnp.float32)  91.8 us
    pmax x1, blocking collectives, local(): logit_max = lax.pmax(jnp.max(logits, axis=1), ('req', 'tp'))  64.1 us
    gather x32, local copies, waits for them, and re-layouts  48.3 us
    all_gather x1, waiting for transfers between devices, local(): lax.all_gather(final_rows, 'req', axis=0, tiled=True)  44.9 us
    dot_general x4, matrix products, per_request(): jnp.einsum('mjl,wml->mjw', query_block, window[..., :head_width], preferr...  16.9 us
    dot_general x5, matrix products, online_update(): jnp.einsum('amz,zav->amv', weight_matrix.astype(jnp.bfloat16), value_matr...  9.56 us
    dot_general x1, matrix products, local(): jnp.dot(lax.all_gather(final_rows, 'req', axis=0, tiled=True), head_weigh...  8.84 us
    dot_general x1, matrix products, local(): jnp.dot(attention, w_out, preferred_element_type=jnp.float32)  7.58 us
  transfers between devices with their start and end apart: 2, of which 2 were waited for; matrix products, arithmetic and copies ran while one was open for 1% of the time, Pallas kernels for 0%

commit v1 on v0

--- a/solution.py
+++ b/solution.py
@@ -169,7 +169,9 @@
     row_norms = jnp.sqrt(jnp.mean(last_rows * last_rows, axis=1) + EPS)
     final_rows = (last_rows / row_norms[:, None] * final_norm_gain[None, :]).astype(jnp.bfloat16)
     logits = jnp.dot(
-        lax.all_gather(final_rows, "req", axis=0, tiled=True),
+        jnp.concatenate(
+            lax.all_to_all(jnp.stack([final_rows] * lax.axis_size("req")), "req", 0, 0), axis=0
+        ),
         head_weight,
         preferred_element_type=jnp.float32,
     )

time: 366 us -> 392 us (1.071)
  waiting for transfers between devices: 137 us -> 150 us
  starting transfers between devices: 0.08 us -> 7.76 us
    all_to_all x0 -> x1, waiting for transfers between devices: none -> 58.5 us  [local(): lax.all_to_all(jnp.stack([final_rows] * lax.axis_size('req')), 'req', 0, 0)]
    all_gather x1 -> x0, waiting for transfers between devices: 44.9 us -> none  [local(): lax.all_gather(final_rows, 'req', axis=0, tiled=True)]
    all_to_all x0 -> x1, starting transfers between devices: none -> 7.72 us  [local(): lax.all_to_all(jnp.stack([final_rows] * lax.axis_size('req')), 'req', 0, 0)]
where the time goes in v1:
time: 392 us; the launch traced here: 391 us
  waiting for transfers between devices  150 us (38%)
  local copies, waits for them, and re-layouts  72.6 us (19%)
  blocking collectives  66.5 us (17%)
  matrix products  51.4 us (13%)
  other arithmetic  27.4 us (7%)
  between operations  14.4 us (4%)
  starting transfers between devices  7.76 us (2%)
    psum x1, waiting for transfers between devices, local(): lax.psum(partial_value.astype(jnp.bfloat16), 'tp').astype(jnp.float32)  91.9 us
    pmax x1, blocking collectives, local(): logit_max = lax.pmax(jnp.max(logits, axis=1), ('req', 'tp'))  66.5 us
    all_to_all x1, waiting for transfers between devices, local(): lax.all_to_all(jnp.stack([final_rows] * lax.axis_size('req')), 'req', 0, 0)  58.5 us
    gather x32, local copies, waits for them, and re-layouts  48.2 us
    dot_general x4, matrix products, per_request(): jnp.einsum('mjl,wml->mjw', query_block, window[..., :head_width], preferr...  16.9 us
    dot_general x5, matrix products, online_update(): jnp.einsum('amz,zav->amv', weight_matrix.astype(jnp.bfloat16), value_matr...  9.57 us
    dot_general x1, matrix products, local(): jnp.dot(jnp.concatenate(lax.all_to_all(jnp.stack([final_rows] * lax.axis_...  8.84 us
  transfers between devices with their start and end apart: 2, of which 2 were waited for; matrix products, arithmetic and copies ran while one was open for 1% of the time, Pallas kernels for 0%

profile of v1, /device:TPU:1, one launch (start us, length us, event | category | flops | bytes accessed | tf_op | source)
XLA Modules:
  0.0 391.1 jit_solution(7699761293110443719)
XLA Ops:
  7.3 3.1 fusion.27
  10.7 3.6 fusion.29
  16.1 4.2 %convolution_add_fusion.1 = f32[384,640]{1,0:T(8,128)} fusion(bf16[384,5120]{1,0:T(8,128)(2,1)S(1)} %fusion.29, bf16[5120,640]{1,0:T(8,128)(2,1)S(1)} %copy-done.12, f32[640]{0:T(1024)S(1)} %copy-done.13), kind=kOutput, calls=%fused_computation.58 | convolution fusion | flops 2516828160 | bytes 11471360 | tf_op jit(solution)/shard_map/dot_general | solution.py:125
  23.5 4.1 %multiply_subtract_fusion = (f32[16,24,1,5,64]{4,3,1,0,2:T(8,128)}, f32[16,24,1,5,64]{4,3,1,0,2:T(8,128)}) fusion(f32[16,24,1,5,128]{4,3,1,0,2:T(8,128)} %reshape.576, f32[16,24,64]{2,1,0:T(8,128)S(1)} %get-tuple-element.120, f32[16,24,64]{2,1,0:T(8,128)S(1)} %get-tuple-element.119), kind=kLoop, calls=%fused_computation.56 | loop fusion | flops 737280 | bytes 2162688 | tf_op jit(solution)/shard_map/sub | solution.py:26
  38.9 3.3 convolution_add_fusion.2
  45.7 80.9 %while.17 = (s32[]{:T(128)}, f32[4,4,1,120]{3,1,2,0:T(4,128)S(1)}, f32[4,4,1,120]{3,1,2,0:T(4,128)S(1)}, f32[4,4,1,120,128]{4,3,1,2,0:T(8,128)}, s32[4,4]{1,0:T(...) while((s32[]{:T(128)}, f32[4,4,1,120]{3,1,2,0:T(4,128)S(1)}, ...), condition=%wide.region_5.6_spmd, body=%wide.region_2.5_spmd.sunk | while | flops 766884224 | bytes 52985684 | solution.py:94
  46.0 12.2 %while.18 = (s32[]{:T(128)}, bf16[26624,1,256]{2,0,1:T(8,128)(2,1)}, s32[4,3]{1,0:T(4,128)S(1)}, bf16[4,3072,1,256]{3,1,2,0:T(8,128)(2,1)}, s32[]{:T(128)}) while((s32[]{:T(128)}, bf16[26624,1,256]{2,0,1:T(8,128)(2,1)}, s32[4,3]{1,0:T(4,128)S(1)}, bf16[4,3072,1,256]{3,1,2,0:T(8,128)(2,1)}, s32[]{:T(128)}) %tuple.62), condition=%wide.while_cond, body=%wide.while_body.sunk | while | flops 2 | bytes 3145833 | solution.py:59
  46.1 3.2 bitcast_dynamic-update-slice_fusion.3
  55.2 3.0 bitcast_dynamic-update-slice_fusion.3
  58.3 4.2 %select_reduce_fusion.2 = (f32[4,120]{1,0:T(4,128)S(1)}, f32[4,120,3072]{2,1,0:T(8,128)S(1)}) fusion(pred[4,3072]{1,0:T(4,128)(4,1)S(1)} %fusion.90, bf16[4,3072,1,256]{3,1,0,2:T(8,128)(2,1)} %bitcast.119, bf16[1,4,1,120,128]{4,1,0,3,2:T(4,128)(2,1)S(1)} %constant_dynamic-slice_fusion.8), kind=kOutput, calls=%fused_computation.3.clone.1 | convolution fusion | flops 380436000 | bytes 9181056 | tf_op jit(solution)/shard_map/while/body/eval_jaxpr/vmap(mjl,wml->mjw)/dot_general | solution.py:62
  66.3 12.0 %while.18 = (s32[]{:T(128)}, bf16[26624,1,256]{2,0,1:T(8,128)(2,1)}, s32[4,3]{1,0:T(4,128)S(1)}, bf16[4,3072,1,256]{3,1,2,0:T(8,128)(2,1)}, s32[]{:T(128)}) while((s32[]{:T(128)}, bf16[26624,1,256]{2,0,1:T(8,128)(2,1)}, s32[4,3]{1,0:T(4,128)S(1)}, bf16[4,3072,1,256]{3,1,2,0:T(8,128)(2,1)}, s32[]{:T(128)}) %tuple.62), condition=%wide.while_cond, body=%wide.while_body.sunk | while | flops 2 | bytes 3145833 | solution.py:59
  75.4 3.0 bitcast_dynamic-update-slice_fusion.3
  78.4 4.2 %select_reduce_fusion.2 = (f32[4,120]{1,0:T(4,128)S(1)}, f32[4,120,3072]{2,1,0:T(8,128)S(1)}) fusion(pred[4,3072]{1,0:T(4,128)(4,1)S(1)} %fusion.90, bf16[4,3072,1,256]{3,1,0,2:T(8,128)(2,1)} %bitcast.119, bf16[1,4,1,120,128]{4,1,0,3,2:T(4,128)(2,1)S(1)} %constant_dynamic-slice_fusion.8), kind=kOutput, calls=%fused_computation.3.clone.1 | convolution fusion | flops 380436000 | bytes 9181056 | tf_op jit(solution)/shard_map/while/body/eval_jaxpr/vmap(mjl,wml->mjw)/dot_general | solution.py:62
  86.5 12.0 %while.18 = (s32[]{:T(128)}, bf16[26624,1,256]{2,0,1:T(8,128)(2,1)}, s32[4,3]{1,0:T(4,128)S(1)}, bf16[4,3072,1,256]{3,1,2,0:T(8,128)(2,1)}, s32[]{:T(128)}) while((s32[]{:T(128)}, bf16[26624,1,256]{2,0,1:T(8,128)(2,1)}, s32[4,3]{1,0:T(4,128)S(1)}, bf16[4,3072,1,256]{3,1,2,0:T(8,128)(2,1)}, s32[]{:T(128)}) %tuple.62), condition=%wide.while_cond, body=%wide.while_body.sunk | while | flops 2 | bytes 3145833 | solution.py:59
  98.5 4.2 %select_reduce_fusion.2 = (f32[4,120]{1,0:T(4,128)S(1)}, f32[4,120,3072]{2,1,0:T(8,128)S(1)}) fusion(pred[4,3072]{1,0:T(4,128)(4,1)S(1)} %fusion.90, bf16[4,3072,1,256]{3,1,0,2:T(8,128)(2,1)} %bitcast.119, bf16[1,4,1,120,128]{4,1,0,3,2:T(4,128)(2,1)S(1)} %constant_dynamic-slice_fusion.8), kind=kOutput, calls=%fused_computation.3.clone.1 | convolution fusion | flops 380436000 | bytes 9181056 | tf_op jit(solution)/shard_map/while/body/eval_jaxpr/vmap(mjl,wml->mjw)/dot_general | solution.py:62
  106.6 12.0 %while.18 = (s32[]{:T(128)}, bf16[26624,1,256]{2,0,1:T(8,128)(2,1)}, s32[4,3]{1,0:T(4,128)S(1)}, bf16[4,3072,1,256]{3,1,2,0:T(8,128)(2,1)}, s32[]{:T(128)}) while((s32[]{:T(128)}, bf16[26624,1,256]{2,0,1:T(8,128)(2,1)}, s32[4,3]{1,0:T(4,128)S(1)}, bf16[4,3072,1,256]{3,1,2,0:T(8,128)(2,1)}, s32[]{:T(128)}) %tuple.62), condition=%wide.while_cond, body=%wide.while_body.sunk | while | flops 2 | bytes 3145833 | solution.py:59
  118.6 4.2 %select_reduce_fusion.2 = (f32[4,120]{1,0:T(4,128)S(1)}, f32[4,120,3072]{2,1,0:T(8,128)S(1)}) fusion(pred[4,3072]{1,0:T(4,128)(4,1)S(1)} %fusion.90, bf16[4,3072,1,256]{3,1,0,2:T(8,128)(2,1)} %bitcast.119, bf16[1,4,1,120,128]{4,1,0,3,2:T(4,128)(2,1)S(1)} %constant_dynamic-slice_fusion.8), kind=kOutput, calls=%fused_computation.3.clone.1 | convolution fusion | flops 380436000 | bytes 9181056 | tf_op jit(solution)/shard_map/while/body/eval_jaxpr/vmap(mjl,wml->mjw)/dot_general | solution.py:62
  129.8 7.6 %convolution_convert_fusion = bf16[384,5120]{1,0:T(8,128)(2,1)} fusion(bf16[384,640]{1,0:T(8,128)(2,1)S(1)} %reshape_transpose_reshape.16, bf16[640,5120]{1,0:T(8,128)(2,1)} %param.18), kind=kOutput, calls=%fused_computation.45 | convolution fusion | flops 2518548480 | bytes 10977280 | tf_op jit(solution)/shard_map/dot_general | solution.py:163
  137.4 91.9 %all-reduce.3.cloned.1.call-done = bf16[384,5120]{1,0:T(8,128)(2,1)} async-done(((bf16[384,5120]{1,0:T(8,128)(2,1)}), bf16[384,5120]{1,0:T(8,128)(2,1)}) %all-reduce.3.cloned.1.call-update) | async-done | bytes 3932176 | tf_op jit(solution)/shard_map/psum | solution.py:165
  229.3 4.8 %fusion.30 = bf16[384,5120]{1,0:T(8,128)(2,1)S(1)} fusion(bf16[384,5120]{1,0:T(8,128)(2,1)} %param.13, bf16[384,5120]{1,0:T(8,128)(2,1)} %all-reduce.3.cloned.1.call-done), kind=kLoop, calls=%fused_computation.44 | loop fusion | flops 7864320 | bytes 11796480 | tf_op jit(solution)/shard_map/convert_element_type | solution.py:166
  239.6 7.7 %all-to-all-start = ((bf16[32,16,5120]{2,1,0:T(8,128)(2,1)}), bf16[32,16,5120]{2,1,0:T(8,128)(2,1)}, u32[]{:S(2)}, u32[]{:S(2)}) async-start(bf16[32,16,5120]{2,1,0:T(8,128)(2,1)} %stack.2), calls=%async_computation | async-start | bytes 10485760 | tf_op jit(solution)/shard_map/all_to_all | solution.py:173
  250.4 58.5 %all-to-all-done = bf16[32,16,5120]{2,1,0:T(8,128)(2,1)} async-done(((bf16[32,16,5120]{2,1,0:T(8,128)(2,1)}), bf16[32,16,5120]{2,1,0:T(8,128)(2,1)}, u32[]{:S(2)}, u32[]{:S(2)}) %all-to-all-start) | async-done | bytes 5242912 | tf_op jit(solution)/shard_map/all_to_all | solution.py:173
  308.9 8.8 %fusion.72 = (f32[512]{0:T(512)S(1)}, f32[512,594]{0,1:T(8,128)}) fusion(bf16[512,5120]{1,0:T(8,128)(2,1)} %bitcast.24, bf16[5120,594]{0,1:T(8,128)(2,1)} %param.21), kind=kOutput, calls=%fused_computation.122 | convolution fusion | flops 3114574336 | bytes 12544000 | tf_op jit(solution)/shard_map/dot_general | solution.py:171
  317.7 66.5 %pmax.7 = f32[512]{0:T(512)} all-reduce(f32[512]{0:T(512)S(1)} %get-tuple-element.123), channel_id=1, replica_groups=mesh['req'=32,'tp'=4] {'req','tp'}, use_global_device_ids=true, to_apply=%region_11.12 | all-reduce | flops 512 | bytes 4096 | tf_op jit(solution)/shard_map/pmax | solution.py:178
  (158 shorter events, 85.9 us)
Async XLA Ops:
  7.2 31.7 %copy-start = (bf16[5120,256]{1,0:T(8,128)(2,1)S(1)}, bf16[5120,256]{1,0:T(8,128)(2,1)}, u32[]{:S(2)}) copy-start(bf16[5120,256]{1,0:T(8,128)(2,1)} %param.16) | copy-start | bytes 7864324
  7.2 3.3 copy-start.10
  7.2 3.5 copy-start.8
  7.2 222.1 %all-reduce.3.cloned.1.call-start = ((), (), s32[]{:S(2)}) async-start(), calls=%async_computation.1 | async-start | bytes 7864320 | tf_op jit(solution)/shard_map/psum | solution.py:165
  10.6 5.5 %copy-start.12 = (bf16[5120,640]{1,0:T(8,128)(2,1)S(1)}, bf16[5120,640]{1,0:T(8,128)(2,1)}, u32[]{:S(2)}) copy-start(bf16[5120,640]{1,0:T(8,128)(2,1)} %param.14) | copy-start | bytes 19660804
  10.7 5.5 %copy-start.13 = (f32[640]{0:T(1024)S(1)}, f32[640]{0:T(1024)}, u32[]{:S(2)}) copy-start(f32[640]{0:T(1024)} %param.15) | copy-start | bytes 7684
  14.2 1.9 copy-start.4
  30.0 8.8 %copy-start.14 = (f32[256]{0:T(256)S(1)}, f32[256]{0:T(256)}, u32[]{:S(2)}) copy-start(f32[256]{0:T(256)} %param.17) | copy-start | bytes 3076
  45.7 81.1 %copy-start.5 = (f32[1920,64]{1,0:T(8,128)S(1)}, f32[1920,64]{1,0:T(8,128)}, u32[]{:S(2)}) copy-start(f32[1920,64]{1,0:T(8,128)} %concatenate.59) | copy-start | bytes 1474564
  45.7 81.1 %copy-start.6 = (f32[1920,64]{1,0:T(8,128)S(1)}, f32[1920,64]{1,0:T(8,128)}, u32[]{:S(2)}) copy-start(f32[1920,64]{1,0:T(8,128)} %concatenate.60) | copy-start | bytes 1474564
  58.3 4.2 %copy-start.2 = (bf16[4,3072,1,256]{3,1,2,0:T(8,128)(2,1)S(1)}, bf16[4,3072,1,256]{3,1,2,0:T(8,128)(2,1)}, u32[]{:S(2)}) copy-start(bf16[4,3072,1,256]{3,1,2,0:T(8,128)(2,1)} %get-tuple-element.216) | copy-start | bytes 18874372 | tf_op jit(solution)/shard_map/while
  78.4 4.3 %copy-start.2 = (bf16[4,3072,1,256]{3,1,2,0:T(8,128)(2,1)S(1)}, bf16[4,3072,1,256]{3,1,2,0:T(8,128)(2,1)}, u32[]{:S(2)}) copy-start(bf16[4,3072,1,256]{3,1,2,0:T(8,128)(2,1)} %get-tuple-element.216) | copy-start | bytes 18874372 | tf_op jit(solution)/shard_map/while
  98.5 4.3 %copy-start.2 = (bf16[4,3072,1,256]{3,1,2,0:T(8,128)(2,1)S(1)}, bf16[4,3072,1,256]{3,1,2,0:T(8,128)(2,1)}, u32[]{:S(2)}) copy-start(bf16[4,3072,1,256]{3,1,2,0:T(8,128)(2,1)} %get-tuple-element.216) | copy-start | bytes 18874372 | tf_op jit(solution)/shard_map/while
  118.6 4.3 %copy-start.2 = (bf16[4,3072,1,256]{3,1,2,0:T(8,128)(2,1)S(1)}, bf16[4,3072,1,256]{3,1,2,0:T(8,128)(2,1)}, u32[]{:S(2)}) copy-start(bf16[4,3072,1,256]{3,1,2,0:T(8,128)(2,1)} %get-tuple-element.216) | copy-start | bytes 18874372 | tf_op jit(solution)/shard_map/while
  126.8 1.5 copy-start.7
  137.4 99.1 %copy-start.9 = (f32[5120]{0:T(1024)S(1)}, f32[5120]{0:T(1024)}, u32[]{:S(2)}) copy-start(f32[5120]{0:T(1024)} %param.20) | copy-start | bytes 61444
  234.1 2.0 copy-start.3
  236.5 3.1 copy-start.11
  239.6 69.2 %all-to-all-start = ((bf16[32,16,5120]{2,1,0:T(8,128)(2,1)}), bf16[32,16,5120]{2,1,0:T(8,128)(2,1)}, u32[]{:S(2)}, u32[]{:S(2)}) async-start(bf16[32,16,5120]{2,1,0:T(8,128)(2,1)} %stack.2), calls=%async_computation | async-start | bytes 10485760 | tf_op jit(solution)/shard_map/all_to_all | solution.py:173
  308.9 75.4 %copy-start.1 = (bf16[5120,256]{1,0:T(8,128)(2,1)S(1)}, bf16[5120,256]{1,0:T(8,128)(2,1)}, u32[]{:S(2)}) copy-start(bf16[5120,256]{1,0:T(8,128)(2,1)} %param.16) | copy-start | bytes 7864324
Sparse Core Ops, SparseCore 0:
  137.5 91.7 all-reduce.2
